TPU v7x, 128 devices: a whole 4x4x4 slice. The times are simulated.
128 devices in a mesh: row: 8 (over x, z_hi), col: 16 (over y, z_lo, core).
Axes of the slice: x: 4, y: 4, z: 4 (z_hi: 2, z_lo: 2; z = z_hi * 2 + z_lo), core: 2. Of those that a mesh axis runs over, the one named last changes fastest.
Arguments:
- grad_out: bfloat16 [16, 256, 8192], P('col', 'row'), may hold values from -0.25 to 0.25
- pre_act: bfloat16 [4096, 14336], P('col', 'row'), may hold values from -6 to 6
- down_weight: bfloat16 [8192, 14336], P('col', 'row'), may hold values from -3 to 3
Outputs:
- grad_pre: bfloat16 [4096, 14336], P('col', 'row')
- grad_weight: bfloat16 [8192, 14336], P('col', 'row')
All inputs are finite; a program needn't handle non-finite values.
Results may differ from a plain program's by a relative error of at most 0.0048.
Values may be sent and summed in bfloat16 or wider, within the bound.
No kernel may reach another device: no remote copies, remote signals or barrier semaphores. Data moves between devices by JAX's collectives and lax.ppermute only.
A program may use at most 128 MiB of HBM per device.

v0:
```python
import math
import jax
import jax.numpy as jnp
from jax import lax
from jax.sharding import PartitionSpec as P


def gelu_parts(pre_float):
    cumulative = 0.5 * (1.0 + jax.scipy.special.erf(pre_float / math.sqrt(2.0)))
    density = jnp.exp(-0.5 * pre_float * pre_float) / math.sqrt(2.0 * math.pi)
    return (pre_float * cumulative, cumulative + pre_float * density)


def shards(grad_out, pre_act, down_weight):
    shard_rows = grad_out[0]
    token_block = lax.all_gather(shard_rows, "row", axis=0, tiled=True)
    column_block = lax.all_to_all(token_block, "col", split_axis=1, concat_axis=0, tiled=True)
    activated, slope = gelu_parts(pre_act.astype(jnp.float32))
    hidden = activated.astype(jnp.bfloat16)
    row_slice = column_block
    grad_hidden = lax.psum_scatter(
        jnp.dot(row_slice, down_weight, preferred_element_type=jnp.float32),
        "col",
        scatter_dimension=0,
        tiled=True,
    )
    grad_pre = (grad_hidden * slope).astype(jnp.bfloat16)
    row_slice = column_block
    grad_weight = lax.dot_general(
        row_slice,
        lax.all_gather(hidden, "col", axis=0, tiled=True),
        (((0,), (0,)), ((), ())),
        preferred_element_type=jnp.float32,
    )
    return (grad_pre, grad_weight.astype(jnp.bfloat16))


def solution(mesh):
    in_specs = (P("col", "row", None), P("col", "row"), P("col", "row"))
    out_specs = (P("col", "row"), P("col", "row"))
    return jax.shard_map(shards, mesh=mesh, in_specs=in_specs, out_specs=out_specs, check_vma=False)
```

profile of v0, /device:TPU:1, one launch (start us, length us, event | category | flops | bytes accessed | tf_op | source)
XLA Modules:
  0.0 583.2 jit_solution(2370361156632593929)
XLA Ops:
  7.2 0.0 copy-start
  7.2 0.0 all-gather.6.cloned.1.call-start
  7.2 0.7 all-gather.6.cloned.1.call-update
  7.9 0.0 reduce-scatter.2.cloned.1.call-start
  8.0 76.8 %all-gather.6.cloned.1.call-done = bf16[1,256,8192]{2,1,0:T(8,128)(2,1)} async-done(((bf16[1,32,8192]{2,1,0:T(8,128)(2,1)}), bf16[1,256,8192]{2,1,0:T(8,128)(2,1)}) %all-gather.6.cloned.1.call-update) | async-done | bytes 4194320 | tf_op jit(solution)/shard_map/all_gather | solution.py:16
  84.8 6.4 %copy.10 = bf16[1,256,8192]{1,2,0:T(8,128)(2,1)} copy(bf16[1,256,8192]{2,1,0:T(8,128)(2,1)} %all-gather.6.cloned.1.call-done) | data formatting | bytes 8388608 | tf_op jit(solution)/shard_map/all_gather | solution.py:16
  91.1 54.5 %all_to_all.19 = bf16[256,16,512]{0,2,1:T(8,128)(2,1)} all-to-all(bf16[256,16,512]{0,2,1:T(8,128)(2,1)} %bitcast.9), channel_id=1, replica_groups=mesh['row'=8,'col'=16] {'col'}, dimensions={1} | all-to-all | bytes 8388608 | tf_op jit(solution)/shard_map/all_to_all | solution.py:17
  145.7 6.4 %copy.11 = bf16[16,256,512]{2,1,0:T(8,128)(2,1)} copy(bf16[16,256,512]{1,2,0:T(8,128)(2,1)} %bitcast.10) | data formatting | bytes 8388608 | tf_op jit(solution)/shard_map/all_to_all | solution.py:17
  152.0 0.0 copy-done
  152.0 16.4 %fusion.10 = f32[4096,1792]{1,0:T(8,128)} fusion(bf16[4096,512]{1,0:T(8,128)(2,1)} %bitcast.11, bf16[512,1792]{1,0:T(8,128)(2,1)S(1)} %copy-done), kind=kOutput, calls=%fused_computation.16 | convolution fusion | flops 7516192768 | bytes 35389440 | tf_op jit(solution)/shard_map/dot_general | solution.py:22
  168.4 0.0 copy-start.2
  168.4 0.0 reduce-scatter.2.cloned.1.call-update
  168.5 0.0 all-gather.4.cloned.1.call-start
  168.5 305.0 %reduce-scatter.2.cloned.1.call-done = f32[256,1792]{1,0:T(8,128)} async-done(((f32[4096,1792]{1,0:T(8,128)}), f32[256,1792]{1,0:T(8,128)}) %reduce-scatter.2.cloned.1.call-update) | async-done | bytes 1835024 | tf_op jit(solution)/shard_map/reduce_scatter | solution.py:21
  473.5 0.0 copy-done.2
  473.5 3.6 fusion.9
  477.1 0.0 all-gather.4.cloned.1.call-update
  477.1 82.4 %all-gather.4.cloned.1.call-done = bf16[4096,1792]{1,0:T(8,128)(2,1)} async-done(((bf16[256,1792]{1,0:T(8,128)(2,1)}), bf16[4096,1792]{1,0:T(8,128)(2,1)}) %all-gather.4.cloned.1.call-update) | async-done | bytes 14680080 | tf_op jit(solution)/shard_map/all_gather | solution.py:31
  559.5 0.0 copy-start.1
  559.5 13.3 %fusion = bf16[512,1792]{0,1:T(8,128)(2,1)} fusion(bf16[4096,1792]{1,0:T(8,128)(2,1)} %all-gather.4.cloned.1.call-done, bf16[4096,512]{1,0:T(8,128)(2,1)} %bitcast.12), kind=kOutput, calls=%fused_computation.6 | convolution fusion | flops 7517110272 | bytes 20709376 | tf_op jit(solution)/shard_map/dot_general | solution.py:29
  572.9 3.8 copy.12
  576.7 0.0 copy-done.1
Async XLA Ops:
  7.2 144.9 %copy-start = (bf16[512,1792]{1,0:T(8,128)(2,1)S(1)}, bf16[512,1792]{1,0:T(8,128)(2,1)}, u32[]{:S(2)}) copy-start(bf16[512,1792]{1,0:T(8,128)(2,1)} %param.5) | copy-start | bytes 5505028
  7.2 77.6 %all-gather.6.cloned.1.call-start = ((), (), s32[]{:S(2)}) async-start(), calls=%async_computation.4 | async-start | bytes 4718592 | tf_op jit(solution)/shard_map/all_gather | solution.py:16
  7.9 465.6 %reduce-scatter.2.cloned.1.call-start = ((), (), s32[]{:S(2)}) async-start(), calls=%async_computation.2 | async-start | bytes 31195136 | tf_op jit(solution)/shard_map/reduce_scatter | solution.py:21
  168.4 305.0 %copy-start.2 = (bf16[256,1792]{1,0:T(8,128)(2,1)S(1)}, bf16[256,1792]{1,0:T(8,128)(2,1)}, u32[]{:S(2)}) copy-start(bf16[256,1792]{1,0:T(8,128)(2,1)} %param.4) | copy-start | bytes 2752516
  168.5 391.1 %all-gather.4.cloned.1.call-start = ((), (), s32[]{:S(2)}) async-start(), calls=%async_computation.3 | async-start | bytes 15597568 | tf_op jit(solution)/shard_map/all_gather | solution.py:31
  559.5 17.1 %copy-start.1 = (bf16[512,1792]{1,0:T(8,128)(2,1)S(1)}, bf16[512,1792]{1,0:T(8,128)(2,1)}, u32[]{:S(2)}) copy-start(bf16[512,1792]{1,0:T(8,128)(2,1)} %param.5) | copy-start | bytes 5505028
Sparse Core Ops, SparseCore 0:
  10.4 74.3 all-gather.5
  168.6 304.8 reduce-scatter.1
  477.2 82.2 all-gather.3
where the time goes:
time: 584 us; the launch traced here: 583 us
  waiting for transfers between devices  465 us (80%)
  blocking collectives  54.5 us (9%)
  matrix products  29.7 us (5%)
  local copies, waits for them, and re-layouts  16.5 us (3%)
  between operations  13.8 us (2%)
    reduce_scatter x1, waiting for transfers between devices, shards(): lax.psum_scatter(jnp.dot(row_slice, down_weight, preferred_element_type=j...  305 us
    all_gather x1, waiting for transfers between devices, shards(): lax.all_gather(hidden, 'col', axis=0, tiled=True)  82.4 us
    all_gather x1, waiting for transfers between devices, shards(): token_block = lax.all_gather(shard_rows, 'row', axis=0, tiled=True)  76.8 us
    all_to_all x1, blocking collectives, shards(): lax.all_to_all(token_block, 'col', split_axis=1, concat_axis=0, tiled=True)  54.5 us
    dot_general x1, matrix products, shards(): jnp.dot(row_slice, down_weight, preferred_element_type=jnp.float32)  16.4 us
    dot_general x1, matrix products, shards(): lax.dot_general(row_slice, lax.all_gather(hidden, 'col', axis=0, tiled=Tr...  13.3 us
  transfers between devices with their start and end apart: 3, of which 3 were waited for; matrix products, arithmetic and copies ran while one was open for 0% of the time, Pallas kernels for 0%

commit v1 on v0

--- a/solution.py
+++ b/solution.py
@@ -13,7 +13,9 @@
 
 def shards(grad_out, pre_act, down_weight):
     shard_rows = grad_out[0]
-    token_block = lax.all_gather(shard_rows, "row", axis=0, tiled=True)
+    token_block = jnp.concatenate(
+        lax.all_to_all(jnp.stack([shard_rows] * lax.axis_size("row")), "row", 0, 0), axis=0
+    )
     column_block = lax.all_to_all(token_block, "col", split_axis=1, concat_axis=0, tiled=True)
     activated, slope = gelu_parts(pre_act.astype(jnp.float32))
     hidden = activated.astype(jnp.bfloat16)

time: 584 us -> 557 us (0.954)
  waiting for transfers between devices: 465 us -> 387 us
  blocking collectives: 54.5 us -> 113 us
    all_gather x1 -> x0, waiting for transfers between devices: 76.8 us -> none  [shards(): token_block = lax.all_gather(shard_rows, 'row', axis=0, tiled=True)]
    all_to_all x0 -> x1, blocking collectives: none -> 57.2 us  [shards(): lax.all_to_all(jnp.stack([shard_rows] * lax.axis_size('row')), 'row', 0, 0)]
    all_gather x1 -> x0, local copies, waits for them, and re-layouts: 6.36 us -> none  [shards(): token_block = lax.all_gather(shard_rows, 'row', axis=0, tiled=True)]
  transfers between devices with their start and end apart: 3 -> 2, of which waited for: 3 -> 2; matrix products, arithmetic and copies ran while one was open for 0% -> 0% of each run, Pallas kernels for 0% -> 0%
where the time goes in v1:
time: 557 us; the launch traced here: 556 us
  waiting for transfers between devices  387 us (69%)
  blocking collectives  113 us (20%)
  matrix products  26.2 us (5%)
  between operations  14.1 us (3%)
  local copies, waits for them, and re-layouts  11.6 us (2%)
    reduce_scatter x1, waiting for transfers between devices, shards(): lax.psum_scatter(jnp.dot(row_slice, down_weight, preferred_element_type=j...  305 us
    all_gather x1, waiting for transfers between devices, shards(): lax.all_gather(hidden, 'col', axis=0, tiled=True)  82.4 us
    all_to_all x1, blocking collectives, shards(): lax.all_to_all(jnp.stack([shard_rows] * lax.axis_size('row')), 'row', 0, 0)  57.2 us
    all_to_all x1, blocking collectives, shards(): lax.all_to_all(token_block, 'col', split_axis=1, concat_axis=0, tiled=True)  56.2 us
    dot_general x1, matrix products, shards(): lax.dot_general(row_slice, lax.all_gather(hidden, 'col', axis=0, tiled=Tr...  13.3 us
    dot_general x1, matrix products, shards(): jnp.dot(row_slice, down_weight, preferred_element_type=jnp.float32)  12.9 us
  transfers between devices with their start and end apart: 2, of which 2 were waited for; matrix products, arithmetic and copies ran while one was open for 0% of the time, Pallas kernels for 0%

profile of v1, /device:TPU:1, one launch (start us, length us, event | category | flops | bytes accessed | tf_op | source)
XLA Modules:
  0.0 556.3 jit_solution(7176272466250472927)
XLA Ops:
  7.2 0.0 copy-start
  7.2 0.0 reduce-scatter.2.cloned.1.call-start
  7.2 1.6 stack.3
  8.9 57.2 %all_to_all.24 = bf16[8,32,8192]{2,1,0:T(8,128)(2,1)S(1)} all-to-all(bf16[8,32,8192]{2,1,0:T(8,128)(2,1)S(1)} %stack.3), channel_id=1, replica_groups=mesh['row'=8,'col'=16] {'row'}, dimensions={0} | all-to-all | bytes 8388608 | tf_op jit(solution)/shard_map/all_to_all | solution.py:17
  66.1 1.9 copy.11
  67.9 2.4 copy.9
  70.3 56.2 %all_to_all.25 = bf16[256,16,512]{2,0,1:T(8,128)(2,1)S(1)} all-to-all(bf16[256,16,512]{2,0,1:T(8,128)(2,1)S(1)} %copy.9), channel_id=1, replica_groups=mesh['row'=8,'col'=16] {'col'}, dimensions={1} | all-to-all | bytes 8388608 | tf_op jit(solution)/shard_map/all_to_all | solution.py:19
  126.5 0.0 copy-start.2
  126.5 1.9 copy-done.2
  128.4 0.0 copy-done
  128.4 12.9 %fusion.10 = f32[4096,1792]{1,0:T(8,128)} fusion(bf16[4096,512]{1,0:T(8,128)(2,1)S(1)} %bitcast.15, bf16[512,1792]{1,0:T(8,128)(2,1)S(1)} %copy-done), kind=kOutput, calls=%fused_computation.16 | convolution fusion | flops 7516192768 | bytes 35389440 | tf_op jit(solution)/shard_map/dot_general | solution.py:24
  141.3 0.0 copy-start.3
  141.3 0.0 reduce-scatter.2.cloned.1.call-update
  141.3 0.0 all-gather.2.cloned.1.call-start
  141.4 305.0 %reduce-scatter.2.cloned.1.call-done = f32[256,1792]{1,0:T(8,128)} async-done(((f32[4096,1792]{1,0:T(8,128)}), f32[256,1792]{1,0:T(8,128)}) %reduce-scatter.2.cloned.1.call-update) | async-done | bytes 1835024 | tf_op jit(solution)/shard_map/reduce_scatter | solution.py:23
  446.3 0.0 copy-done.3
  446.3 3.6 fusion.9
  449.9 0.0 all-gather.2.cloned.1.call-update
  450.0 82.4 %all-gather.2.cloned.1.call-done = bf16[4096,1792]{1,0:T(8,128)(2,1)} async-done(((bf16[256,1792]{1,0:T(8,128)(2,1)}), bf16[4096,1792]{1,0:T(8,128)(2,1)}) %all-gather.2.cloned.1.call-update) | async-done | bytes 14680080 | tf_op jit(solution)/shard_map/all_gather | solution.py:33
  532.4 0.0 copy-start.1
  532.4 13.3 %fusion = bf16[512,1792]{0,1:T(8,128)(2,1)} fusion(bf16[4096,1792]{1,0:T(8,128)(2,1)} %all-gather.2.cloned.1.call-done, bf16[4096,512]{1,0:T(8,128)(2,1)} %bitcast.16), kind=kOutput, calls=%fused_computation.6 | convolution fusion | flops 7517110272 | bytes 20709376 | tf_op jit(solution)/shard_map/dot_general | solution.py:31
  545.7 3.8 copy.10
  549.5 0.0 copy-done.1
Async XLA Ops:
  7.2 121.3 %copy-start = (bf16[512,1792]{1,0:T(8,128)(2,1)S(1)}, bf16[512,1792]{1,0:T(8,128)(2,1)}, u32[]{:S(2)}) copy-start(bf16[512,1792]{1,0:T(8,128)(2,1)} %param.5) | copy-start | bytes 5505028
  7.2 439.1 %reduce-scatter.2.cloned.1.call-start = ((), (), s32[]{:S(2)}) async-start(), calls=%async_computation.3 | async-start | bytes 31195136 | tf_op jit(solution)/shard_map/reduce_scatter | solution.py:23
  126.5 1.9 copy-start.2
  141.3 305.0 %copy-start.3 = (bf16[256,1792]{1,0:T(8,128)(2,1)S(1)}, bf16[256,1792]{1,0:T(8,128)(2,1)}, u32[]{:S(2)}) copy-start(bf16[256,1792]{1,0:T(8,128)(2,1)} %param.4) | copy-start | bytes 2752516
  141.3 391.1 %all-gather.2.cloned.1.call-start = ((), (), s32[]{:S(2)}) async-start(), calls=%async_computation.4 | async-start | bytes 15597568 | tf_op jit(solution)/shard_map/all_gather | solution.py:33
  532.4 17.1 %copy-start.1 = (bf16[512,1792]{1,0:T(8,128)(2,1)S(1)}, bf16[512,1792]{1,0:T(8,128)(2,1)}, u32[]{:S(2)}) copy-start(bf16[512,1792]{1,0:T(8,128)(2,1)} %param.5) | copy-start | bytes 5505028
Sparse Core Ops, SparseCore 0:
  141.4 304.8 reduce-scatter.1
  450.1 82.2 all-gather.1
